TPU v7x, 128 devices: a whole 4x4x4 slice. The times are simulated.
128 devices in a mesh: cache: 32 (over y, z, core), cand: 4 (over x).
Axes of the slice: x: 4, y: 4, z: 4, core: 2. Of those that a mesh axis runs over, the one named last changes fastest.
Arguments:
- cand_states: bfloat16 [1024, 64, 1024], P('cand', 'cache'), may hold values from -6 to 6
- in_proj: bfloat16 [1024, 4, 1024], P(None, None, 'cand'), may hold values from -0.1875 to 0.1875
- out_proj: bfloat16 [1024, 1024], P('cand'), may hold values from -0.1875 to 0.1875
- history: bfloat16 [32, 64, 2, 128, 1024], P('cache', None, None, None, 'cand'), may hold values from -6 to 6
- lengths: int32 [64], replicated, may hold values from 2048 to 4096, as said below
- rank_users: int32 [64], replicated, may hold values from 0 to 63, each once
- recency_bias: float32 [8, 14], P('cand'), may hold values from -4 to 4
- score_weight: float32 [1024], replicated, may hold values from -0.1875 to 0.1875
Outputs:
- layer_out: bfloat16 [1024, 64, 1024], P('cand', 'cache')
- scores: float32 [1024, 64], P('cand', 'cache')
Inputs may be any that keep to these rules, and one draw needn't show every extreme that they name: `lengths`: every length is a multiple of 128; some user's length is exactly 4096. `rank_users`: each user is ranked in exactly one slot.
All inputs are finite; a program needn't handle non-finite values.
Results may differ from a plain program's by a relative error of at most 0.008.
Values may be sent and summed in bfloat16 or wider, within the bound.
A program may use at most 128 MiB of HBM per device.

v0:
```python
import math

import jax
import jax.numpy as jnp
from jax import lax
from jax.sharding import PartitionSpec as P

BLOCK = 128


EPSILON = 1e-06


def laid_out(tiles, dim):
    tiles = jnp.moveaxis(tiles, 0, dim)
    lengths = tiles.shape
    return tiles.reshape(*lengths[:dim], lengths[dim] * lengths[dim + 1], *lengths[dim + 2 :])


def work_in_pieces(array, axis, dim, apply, out_dim):
    size, rows = (lax.axis_size(axis), array.shape[dim])
    count = 2 if rows % 2 == 0 else 1
    done, length = ([], rows // count)
    for k in range(count):
        piece = lax.slice_in_dim(array, k * length, (k + 1) * length, axis=dim)
        starts = jnp.arange(size) * rows + k * length
        done.append(jax.vmap(apply)(lax.all_gather(piece, axis), starts))
    return laid_out(jnp.concatenate(done, axis=out_dim + 1), out_dim)


def bucket_index(distance, bucket_count):
    powers = 2 ** jnp.arange(bucket_count - 1, dtype=jnp.int32)
    return jnp.sum((distance[..., None] >= powers).astype(jnp.int32), axis=-1)


def local(cand_states, in_proj, out_proj, history, lengths, rank_users, recency_bias, score_weight):
    cache_count = lax.axis_size("cache")
    my_group = lax.axis_index("cache")
    cand_rows, users_here, width = cand_states.shape
    head_width = in_proj.shape[2]
    heads_here, bucket_count = recency_bias.shape
    head_size = head_width // heads_here
    scale = head_size ** (-0.5)
    float_states = cand_states.astype(jnp.float32)
    normed = (
        float_states
        * lax.rsqrt(jnp.mean(float_states * float_states, axis=-1, keepdims=True) + EPSILON)
    ).astype(jnp.bfloat16)
    proj_matrix = in_proj.reshape(width, 4 * head_width)

    def project(shard_rows, first_row):
        row_count = shard_rows.shape[0]
        product = jnp.dot(
            shard_rows.reshape(row_count * users_here, width),
            proj_matrix,
            preferred_element_type=jnp.float32,
        )
        return (
            jax.nn.silu(product).astype(jnp.bfloat16).reshape(row_count, users_here, 4, head_width)
        )

    projected = work_in_pieces(normed, "cand", 0, project, 0)
    all_cands = projected.shape[0]
    stored = history[0]
    page_events = stored.shape[2]
    chosen = jnp.take(stored, rank_users, axis=0).reshape(
        cache_count, users_here, 2, page_events, head_width
    )
    arrived = lax.all_to_all(chosen, "cache", split_axis=0, concat_axis=0, tiled=True)
    total_events = cache_count * page_events
    key_block = min(1024, total_events)
    group = math.gcd(cache_count, max(1, key_block // BLOCK))
    groups = cache_count // group
    block_rows = group * BLOCK
    span = cache_count * BLOCK
    my_users = lax.dynamic_slice_in_dim(rank_users, my_group * users_here, users_here)
    my_lengths = jnp.take(lengths, my_users)
    local_rows = jnp.arange(block_rows, dtype=jnp.int32)
    bucket_ids = jnp.arange(bucket_count, dtype=jnp.int32)
    bias_columns = recency_bias.T

    def attend_user(member, gated):
        user = my_users[member]
        length = my_lengths[member]
        own = lax.dynamic_index_in_dim(projected, member, 1, keepdims=False)
        gates = own[:, 0].reshape(all_cands, heads_here, head_size)
        own_values = own[:, 1].reshape(all_cands, heads_here, head_size)
        queries = own[:, 2].reshape(all_cands, heads_here, head_size)
        own_keys = own[:, 3].reshape(all_cands, heads_here, head_size)

        def add_block(step, totals):
            page_block = step // groups
            first_shard = step % groups * group
            piece = lax.dynamic_slice(
                arrived,
                (first_shard, member, 0, page_block * BLOCK, 0),
                (group, 1, 2, BLOCK, head_width),
            )
            block_keys = piece[:, 0, 0].reshape(block_rows, heads_here, head_size)
            block_values = piece[:, 0, 1].reshape(block_rows, heads_here, head_size)
            shard_of_row = first_shard + local_rows // BLOCK
            positions = (
                page_block * cache_count + jnp.remainder(shard_of_row - user, cache_count)
            ) * BLOCK + local_rows % BLOCK
            usable = positions < length
            distance = jnp.maximum(length - positions, 0)
            onehot = (bucket_index(distance, bucket_count)[:, None] == bucket_ids[None, :]).astype(
                jnp.float32
            )
            block_bias = jnp.dot(onehot, bias_columns, precision=lax.Precision.HIGHEST)
            scores = (
                jnp.einsum("chd,khd->chk", queries, block_keys, preferred_element_type=jnp.float32)
                * scale
                + block_bias.T[None]
            )
            weights = jnp.where(usable[None, None, :], jax.nn.silu(scores), 0.0).astype(
                jnp.bfloat16
            )
            return totals + jnp.einsum(
                "chk,khd->chd", weights, block_values, preferred_element_type=jnp.float32
            )

        used_steps = (length + span - 1) // span * groups
        totals = lax.fori_loop(
            0, used_steps, add_block, jnp.zeros((all_cands, heads_here, head_size), jnp.float32)
        )
        self_scores = (
            jnp.sum(queries.astype(jnp.float32) * own_keys.astype(jnp.float32), axis=-1) * scale
            + recency_bias[:, 0][None, :]
        )
        totals = totals + jax.nn.silu(self_scores)[..., None] * own_values.astype(jnp.float32)
        normalized = totals * lax.rsqrt(jnp.mean(totals * totals, axis=-1, keepdims=True) + EPSILON)
        result = (
            (normalized * gates.astype(jnp.float32))
            .astype(jnp.bfloat16)
            .reshape(all_cands, 1, head_width)
        )
        return lax.dynamic_update_slice_in_dim(gated, result, member, 1)

    gated = lax.fori_loop(
        0, users_here, attend_user, jnp.zeros((all_cands, users_here, head_width), jnp.bfloat16)
    )
    spread = lax.all_to_all(gated, "cand", split_axis=0, concat_axis=2, tiled=True)
    full_out = lax.all_gather(out_proj, "cand", axis=0, tiled=True)
    branch_sum = jnp.dot(
        spread.reshape(cand_rows * users_here, width), full_out, preferred_element_type=jnp.float32
    ).reshape(cand_rows, users_here, width)
    layer_sum = float_states + branch_sum
    scores_out = jnp.sum(layer_sum * score_weight, axis=-1)
    return (layer_sum.astype(jnp.bfloat16), scores_out)


def solution(mesh):
    in_specs = (
        P("cand", "cache", None),
        P(None, None, "cand"),
        P("cand", None),
        P("cache", None, None, None, "cand"),
        P(),
        P(),
        P("cand", None),
        P(),
    )
    out_specs = (P("cand", "cache", None), P("cand", "cache"))
    return jax.shard_map(local, mesh=mesh, in_specs=in_specs, out_specs=out_specs, check_vma=False)
```

profile of v0, /device:TPU:32, one launch (start us, length us, event | category | flops | bytes accessed | tf_op | source)
XLA Modules:
  0.0 318.9 jit_solution(15701432249067152249)
XLA Ops:
  7.2 1.6 fusion.59
  8.8 1.5 fusion.60
  11.6 8.9 %gather_fusion.1 = bf16[64,2,128,256]{3,2,1,0:T(8,128)(2,1)} fusion(bf16[64,2,128,256]{3,2,1,0:T(8,128)(2,1)} %bitcast.123, s32[1024]{0:T(1024)S(1)} %pad_clamp_fusion), kind=kCustom, calls=%fused_computation.1 | custom fusion | bytes 16777472 | tf_op jit(solution)/shard_map/jit(_take)/gather | solution.py:66
  20.6 7.8 %broadcast_select_fusion = bf16[32,2,2,128,256]{4,3,2,1,0:T(8,128)(2,1)} fusion(bf16[32,2,2,128,256]{4,3,2,1,0:T(8,128)(2,1)} %bitcast.122, pred[32,2]{1,0:T(8,128)(4,1)S(1)} %broadcast_in_dim.60), kind=kLoop, calls=%fused_computation.93 | loop fusion | flops 4194304 | bytes 16777280 | tf_op jit(solution)/shard_map/jit(_take)/select_n | solution.py:66
  28.4 8.5 %all-to-all-start = ((bf16[32,2,2,128,256]{4,3,2,1,0:T(8,128)(2,1)}), bf16[32,2,2,128,256]{4,3,2,1,0:T(8,128)(2,1)}, u32[]{:S(2)}, u32[]{:S(2)}) async-start(bf16[32,2,2,128,256]{4,3,2,1,0:T(8,128)(2,1)} %broadcast_select_fusion), calls=%async_computation | async-start | bytes 16777216 | tf_op jit(solution)/shard_map/all_to_all | solution.py:69
  38.4 2.7 reshape.332
  42.0 2.4 all-gather.8.cloned.1.call-done
  44.4 3.7 %copy.46 = bf16[512,2,1024]{2,1,0:T(2,128)(2,1)S(1)} copy(bf16[512,2,1024]{2,0,1:T(8,128)(2,1)} %all-gather.8.cloned.1.call-done) | data formatting | bytes 4194304 | tf_op jit(solution)/shard_map/all_gather | solution.py:27
  48.1 2.2 reshape.296
  50.3 4.9 %multiply_convert_fusion.1 = bf16[4,256,1024]{2,1,0:T(8,128)(2,1)S(1)} fusion(bf16[4,256,1024]{2,1,0:T(8,128)(2,1)} %reshape.296, bf16[1024,1024,1]{1,0,2:T(8,128)(2,1)} %reshape.332), kind=kOutput, calls=%fused_computation.96 | convolution fusion | flops 2152726528 | bytes 6291456 | tf_op jit(solution)/shard_map/vmap()/dot_general | solution.py:53
  55.3 2.8 reshape.298
  58.0 18.8 %all-gather.10.cloned.1.call-done = bf16[512,2,1024]{2,0,1:T(8,128)(2,1)} async-done(((bf16[128,2,1024]{2,0,1:T(8,128)(2,1)}), bf16[512,2,1024]{2,0,1:T(8,128)(2,1)}) %all-gather.10.cloned.1.call-update) | async-done | bytes 2097168 | tf_op jit(solution)/shard_map/all_gather | solution.py:27
  76.8 3.7 %copy.47 = bf16[512,2,1024]{2,1,0:T(2,128)(2,1)S(1)} copy(bf16[512,2,1024]{2,0,1:T(8,128)(2,1)} %all-gather.10.cloned.1.call-done) | data formatting | bytes 4194304 | tf_op jit(solution)/shard_map/all_gather | solution.py:27
  80.6 2.3 reshape.299
  82.9 6.3 %multiply_convert_fusion = bf16[4,256,1024]{2,1,0:T(8,128)(2,1)} fusion(bf16[4,256,1024]{2,1,0:T(8,128)(2,1)} %reshape.299, bf16[1024,1024,1]{1,0,2:T(8,128)(2,1)} %reshape.332), kind=kOutput, calls=%fused_computation.95 | convolution fusion | flops 2152726528 | bytes 6291456 | tf_op jit(solution)/shard_map/vmap()/dot_general | solution.py:53
  89.2 4.7 %reshape.300 = bf16[4,128,2,4,256]{4,3,2,1,0:T(4,128)(2,1)} reshape(bf16[4,256,1024]{2,1,0:T(8,128)(2,1)} %multiply_convert_fusion) | data formatting | bytes 4194304 | tf_op jit(solution)/shard_map/vmap()/reshape | solution.py:59
  93.9 6.3 %pad_maximum_fusion = bf16[4,256,2,4,256]{4,3,2,1,0:T(4,128)(2,1)} fusion(bf16[4,128,2,4,256]{4,3,2,1,0:T(4,128)(2,1)} %reshape.300, bf16[4,128,2,4,256]{4,3,2,1,0:T(4,128)(2,1)S(1)} %copy-done.3), kind=kLoop, calls=%fused_computation.94 | loop fusion | flops 2097152 | bytes 8388608 | tf_op jit(solution)/shard_map/concatenate | solution.py:28
  100.1 60.9 %all-to-all-done = bf16[32,2,2,128,256]{4,3,2,1,0:T(8,128)(2,1)} async-done(((bf16[32,2,2,128,256]{4,3,2,1,0:T(8,128)(2,1)}), bf16[32,2,2,128,256]{4,3,2,1,0:T(8,128)(2,1)}, u32[]{:S(2)}, u32[]{:S(2)}) %all-to-all-start) | async-done | bytes 8388640 | tf_op jit(solution)/shard_map/all_to_all | solution.py:69
  161.1 14.7 %copy.49 = bf16[32,2,2,128,256]{3,0,4,2,1:T(8,128)(2,1)} copy(bf16[32,2,2,128,256]{4,3,2,1,0:T(8,128)(2,1)} %all-to-all-done) | data formatting | bytes 16777216
  175.8 107.7 %while.69 = (s32[]{:T(128)}, bf16[1024,2,256]{0,2,1:T(8,128)(2,1)}, s32[2]{0:T(128)S(1)}, s32[2]{0:T(128)S(1)}, bf16[1024,2,4,256]{3,2,1,0:T(4,128)(2,1)}, /*ind...) while((s32[]{:T(128)}, bf16[1024,2,256]{0,2,1:T(8,128)(2,1)}, ...), condition=%wide.region_7.8_spmd.clone.clone, body=%wide.region_1.7_spmd.clone.clone.sunk | while | flops 1095471488 | bytes 39493176 | solution.py:140
  177.0 3.7 %constant_dynamic-slice_fusion.5 = bf16[1024,1,4,256]{3,2,1,0:T(4,128)(2,1)} fusion(bf16[1024,2,4,256]{3,2,1,0:T(4,128)(2,1)} %get-tuple-element.1478, s32[]{:T(128)} %get-tuple-element.1450), kind=kLoop, calls=%fused_computation.92.clone.1 | loop fusion | bytes 4194308 | tf_op jit(solution)/shard_map/while/body/eval_jaxpr/jit(dynamic_index_in_dim)/dynamic_slice | solution.py:85
  180.7 3.0 copy.65
  186.6 38.8 %while.70 = (s32[]{:T(128)}, f32[1024,2,128]{0,2,1:T(8,128)S(1)}, s32[]{:T(128)}, bf16[32,2,2,128,256]{3,0,4,2,1:T(8,128)(2,1)}, s32[]{:T(128)}, /*index=5*/s32[...) while((s32[]{:T(128)}, f32[1024,2,128]{0,2,1:T(8,128)S(1)}, ...), condition=%wide.region_4.4_spmd.clone, body=%wide.region_2.3_spmd.clone.sunk | while | flops 1091259776 | bytes 7936794 | solution.py:124
  186.7 1.3 constant_dynamic-slice_fusion.6
  191.6 4.7 %fusion.99 = f32[1024,2,128]{0,2,1:T(8,128)S(1)} fusion(f32[1024,2,128]{0,2,1:T(8,128)S(1)} %get-tuple-element.1377, bf16[1024,2,128]{0,2,1:T(8,128)(2,1)S(1)} %squeeze.138, f32[2,1024]{1,0:T(2,128)S(1)} %convolution_bitcast_fusion.2, pred[1024]{0:T(1024)(128)(4,1)S(1)} %fusion.98, bf16[1024,2,128]{0,2,1:T(8,128)(2,1)S(1)} %squeeze.139, ...), kind=kOutput, calls=%fused_computation.19.clone.1 | convolution fusion | flops 1090781184 | bytes 3679232 | tf_op jit(solution)/shard_map/while/body/eval_jaxpr/while/body/chk,khd->chd/dot_general | solution.py:119
  196.4 1.3 constant_dynamic-slice_fusion.6
  201.3 4.7 %fusion.99 = f32[1024,2,128]{0,2,1:T(8,128)S(1)} fusion(f32[1024,2,128]{0,2,1:T(8,128)S(1)} %get-tuple-element.1377, bf16[1024,2,128]{0,2,1:T(8,128)(2,1)S(1)} %squeeze.138, f32[2,1024]{1,0:T(2,128)S(1)} %convolution_bitcast_fusion.2, pred[1024]{0:T(1024)(128)(4,1)S(1)} %fusion.98, bf16[1024,2,128]{0,2,1:T(8,128)(2,1)S(1)} %squeeze.139, ...), kind=kOutput, calls=%fused_computation.19.clone.1 | convolution fusion | flops 1090781184 | bytes 3679232 | tf_op jit(solution)/shard_map/while/body/eval_jaxpr/while/body/chk,khd->chd/dot_general | solution.py:119
  206.1 1.3 constant_dynamic-slice_fusion.6
  211.0 4.7 %fusion.99 = f32[1024,2,128]{0,2,1:T(8,128)S(1)} fusion(f32[1024,2,128]{0,2,1:T(8,128)S(1)} %get-tuple-element.1377, bf16[1024,2,128]{0,2,1:T(8,128)(2,1)S(1)} %squeeze.138, f32[2,1024]{1,0:T(2,128)S(1)} %convolution_bitcast_fusion.2, pred[1024]{0:T(1024)(128)(4,1)S(1)} %fusion.98, bf16[1024,2,128]{0,2,1:T(8,128)(2,1)S(1)} %squeeze.139, ...), kind=kOutput, calls=%fused_computation.19.clone.1 | convolution fusion | flops 1090781184 | bytes 3679232 | tf_op jit(solution)/shard_map/while/body/eval_jaxpr/while/body/chk,khd->chd/dot_general | solution.py:119
  215.8 1.3 constant_dynamic-slice_fusion.6
  220.7 4.7 %fusion.99 = f32[1024,2,128]{0,2,1:T(8,128)S(1)} fusion(f32[1024,2,128]{0,2,1:T(8,128)S(1)} %get-tuple-element.1377, bf16[1024,2,128]{0,2,1:T(8,128)(2,1)S(1)} %squeeze.138, f32[2,1024]{1,0:T(2,128)S(1)} %convolution_bitcast_fusion.2, pred[1024]{0:T(1024)(128)(4,1)S(1)} %fusion.98, bf16[1024,2,128]{0,2,1:T(8,128)(2,1)S(1)} %squeeze.139, ...), kind=kOutput, calls=%fused_computation.19.clone.1 | convolution fusion | flops 1090781184 | bytes 3679232 | tf_op jit(solution)/shard_map/while/body/eval_jaxpr/while/body/chk,khd->chd/dot_general | solution.py:119
  225.4 1.5 fusion.89
  227.2 1.3 fusion.90
  230.8 3.7 %constant_dynamic-slice_fusion.5 = bf16[1024,1,4,256]{3,2,1,0:T(4,128)(2,1)} fusion(bf16[1024,2,4,256]{3,2,1,0:T(4,128)(2,1)} %get-tuple-element.1478, s32[]{:T(128)} %get-tuple-element.1450), kind=kLoop, calls=%fused_computation.92.clone.1 | loop fusion | bytes 4194308 | tf_op jit(solution)/shard_map/while/body/eval_jaxpr/jit(dynamic_index_in_dim)/dynamic_slice | solution.py:85
  234.5 3.0 copy.65
  240.5 38.8 %while.70 = (s32[]{:T(128)}, f32[1024,2,128]{0,2,1:T(8,128)S(1)}, s32[]{:T(128)}, bf16[32,2,2,128,256]{3,0,4,2,1:T(8,128)(2,1)}, s32[]{:T(128)}, /*index=5*/s32[...) while((s32[]{:T(128)}, f32[1024,2,128]{0,2,1:T(8,128)S(1)}, ...), condition=%wide.region_4.4_spmd.clone, body=%wide.region_2.3_spmd.clone.sunk | while | flops 1091259776 | bytes 7936794 | solution.py:124
  240.5 1.3 constant_dynamic-slice_fusion.6
  245.5 4.7 %fusion.99 = f32[1024,2,128]{0,2,1:T(8,128)S(1)} fusion(f32[1024,2,128]{0,2,1:T(8,128)S(1)} %get-tuple-element.1377, bf16[1024,2,128]{0,2,1:T(8,128)(2,1)S(1)} %squeeze.138, f32[2,1024]{1,0:T(2,128)S(1)} %convolution_bitcast_fusion.2, pred[1024]{0:T(1024)(128)(4,1)S(1)} %fusion.98, bf16[1024,2,128]{0,2,1:T(8,128)(2,1)S(1)} %squeeze.139, ...), kind=kOutput, calls=%fused_computation.19.clone.1 | convolution fusion | flops 1090781184 | bytes 3679232 | tf_op jit(solution)/shard_map/while/body/eval_jaxpr/while/body/chk,khd->chd/dot_general | solution.py:119
  250.2 1.3 constant_dynamic-slice_fusion.6
  255.2 4.7 %fusion.99 = f32[1024,2,128]{0,2,1:T(8,128)S(1)} fusion(f32[1024,2,128]{0,2,1:T(8,128)S(1)} %get-tuple-element.1377, bf16[1024,2,128]{0,2,1:T(8,128)(2,1)S(1)} %squeeze.138, f32[2,1024]{1,0:T(2,128)S(1)} %convolution_bitcast_fusion.2, pred[1024]{0:T(1024)(128)(4,1)S(1)} %fusion.98, bf16[1024,2,128]{0,2,1:T(8,128)(2,1)S(1)} %squeeze.139, ...), kind=kOutput, calls=%fused_computation.19.clone.1 | convolution fusion | flops 1090781184 | bytes 3679232 | tf_op jit(solution)/shard_map/while/body/eval_jaxpr/while/body/chk,khd->chd/dot_general | solution.py:119
  264.9 4.7 %fusion.99 = f32[1024,2,128]{0,2,1:T(8,128)S(1)} fusion(f32[1024,2,128]{0,2,1:T(8,128)S(1)} %get-tuple-element.1377, bf16[1024,2,128]{0,2,1:T(8,128)(2,1)S(1)} %squeeze.138, f32[2,1024]{1,0:T(2,128)S(1)} %convolution_bitcast_fusion.2, pred[1024]{0:T(1024)(128)(4,1)S(1)} %fusion.98, bf16[1024,2,128]{0,2,1:T(8,128)(2,1)S(1)} %squeeze.139, ...), kind=kOutput, calls=%fused_computation.19.clone.1 | convolution fusion | flops 1090781184 | bytes 3679232 | tf_op jit(solution)/shard_map/while/body/eval_jaxpr/while/body/chk,khd->chd/dot_general | solution.py:119
  274.6 4.7 %fusion.99 = f32[1024,2,128]{0,2,1:T(8,128)S(1)} fusion(f32[1024,2,128]{0,2,1:T(8,128)S(1)} %get-tuple-element.1377, bf16[1024,2,128]{0,2,1:T(8,128)(2,1)S(1)} %squeeze.138, f32[2,1024]{1,0:T(2,128)S(1)} %convolution_bitcast_fusion.2, pred[1024]{0:T(1024)(128)(4,1)S(1)} %fusion.98, bf16[1024,2,128]{0,2,1:T(8,128)(2,1)S(1)} %squeeze.139, ...), kind=kOutput, calls=%fused_computation.19.clone.1 | convolution fusion | flops 1090781184 | bytes 3679232 | tf_op jit(solution)/shard_map/while/body/eval_jaxpr/while/body/chk,khd->chd/dot_general | solution.py:119
  279.3 1.5 fusion.89
  281.1 1.3 fusion.90
  283.5 2.6 copy.51
  286.1 18.9 %all_to_all.20 = bf16[1024,2,256]{2,1,0:T(2,128)(2,1)S(1)} all-to-all(bf16[1024,2,256]{2,1,0:T(2,128)(2,1)S(1)} %copy.51), channel_id=1, replica_groups=mesh['cache'=32,'cand'=4] {'cand'}, dimensions={0} | all-to-all | bytes 2097152 | tf_op jit(solution)/shard_map/all_to_all | solution.py:143
  306.6 3.7 %multiply_reduce_fusion.1 = (f32[256,2]{0,1:T(2,128)}, bf16[256,2,1024]{2,0,1:T(8,128)(2,1)S(1)}) fusion(f32[1024]{0:T(1024)S(1)} %copy-done.10, bf16[256,2,1024]{2,0,1:T(8,128)(2,1)S(1)} %dot_general.31, bf16[1024,1024]{1,0:T(8,128)(2,1)} %all-gather.6.cloned.1.call-done, bf16[256,2,1024]{2,1,0:T(2,128)(2,1)S(1)} %copy-done.4), kind=kOutput, calls=%fused_computation.104 | convolution fusion | flops 1076362752 | bytes 5249024 | tf_op jit(solution)/shard_map/dot_general | solution.py:145
  310.3 2.0 copy.53
  (153 shorter events, 46.4 us)
Async XLA Ops:
  7.2 34.2 %copy-start = (s32[64]{0:T(128)S(1)}, s32[64]{0:T(128)}, u32[]{:S(2)}) copy-start(s32[64]{0:T(128)} %param.16) | copy-start | bytes 772
  7.2 4.3 %copy-start.9 = (s32[64]{0:T(128)S(1)}, s32[64]{0:T(128)}, u32[]{:S(2)}) copy-start(s32[64]{0:T(128)} %param.17) | copy-start | bytes 772
  7.2 37.2 %all-gather.8.cloned.1.call-start = ((), (), s32[]{:S(2)}) async-start(), calls=%async_computation.3 | async-start | bytes 2621440 | tf_op jit(solution)/shard_map/all_gather | solution.py:27
  28.4 10.1 %copy-start.5 = (bf16[1024,4,256]{2,1,0:T(4,128)(2,1)S(1)}, bf16[1024,4,256]{2,1,0:T(4,128)(2,1)}, u32[]{:S(2)}) copy-start(bf16[1024,4,256]{2,1,0:T(4,128)(2,1)} %param.13) | copy-start | bytes 6291460
  28.4 132.7 %all-to-all-start = ((bf16[32,2,2,128,256]{4,3,2,1,0:T(8,128)(2,1)}), bf16[32,2,2,128,256]{4,3,2,1,0:T(8,128)(2,1)}, u32[]{:S(2)}, u32[]{:S(2)}) async-start(bf16[32,2,2,128,256]{4,3,2,1,0:T(8,128)(2,1)} %broadcast_select_fusion), calls=%async_computation | async-start | bytes 16777216 | tf_op jit(solution)/shard_map/all_to_all | solution.py:69
  36.9 4.2 %copy-start.8 = (f32[2,14]{1,0:T(2,128)S(1)}, f32[2,14]{1,0:T(2,128)}, u32[]{:S(2)}) copy-start(f32[2,14]{1,0:T(2,128)} %param.18) | copy-start | bytes 340
  36.9 39.9 %all-gather.10.cloned.1.call-start = ((), (), s32[]{:S(2)}) async-start(), calls=%async_computation.4 | async-start | bytes 2621440 | tf_op jit(solution)/shard_map/all_gather | solution.py:27
  37.7 268.9 %all-gather.6.cloned.1.call-start = ((), (), s32[]{:S(2)}) async-start(), calls=%async_computation.2 | async-start | bytes 2621440 | tf_op jit(solution)/shard_map/all_gather | solution.py:144
  89.2 4.7 %copy-start.3 = (bf16[4,128,2,4,256]{4,3,2,1,0:T(4,128)(2,1)S(1)}, bf16[4,128,2,4,256]{4,3,2,1,0:T(4,128)(2,1)}, u32[]{:S(2)}) copy-start(bf16[4,128,2,4,256]{4,3,2,1,0:T(4,128)(2,1)} %reshape.298) | copy-start | bytes 6291460
  184.8 1.8 copy-start.2
  225.4 3.2 copy-start.6
  228.6 1.0 copy-start.7
  238.7 1.8 copy-start.2
  279.3 3.2 copy-start.6
  282.5 1.0 copy-start.7
  283.5 23.1 %copy-start.4 = (bf16[256,2,1024]{2,1,0:T(2,128)(2,1)S(1)}, bf16[256,2,1024]{2,1,0:T(2,128)(2,1)}, u32[]{:S(2)}) copy-start(bf16[256,2,1024]{2,1,0:T(2,128)(2,1)} %param.12) | copy-start | bytes 3145732
  283.5 23.1 %copy-start.10 = (f32[1024]{0:T(1024)S(1)}, f32[1024]{0:T(1024)}, u32[]{:S(2)}) copy-start(f32[1024]{0:T(1024)} %param.19) | copy-start | bytes 12292
  305.8 6.6 %copy-start.1 = (s32[64]{0:T(128)S(1)}, s32[64]{0:T(128)}, u32[]{:S(2)}) copy-start(s32[64]{0:T(128)} %param.16) | copy-start | bytes 772
Sparse Core Ops, SparseCore 0:
  11.6 32.7 all-gather.7
  46.0 30.7 all-gather.9
  78.5 30.7 all-gather.5
where the time goes:
time: 321 us; the launch traced here: 319 us
  local copies, waits for them, and re-layouts  90.3 us (28%)
  waiting for transfers between devices  83.4 us (26%)
  matrix products  56 us (17%)
  other arithmetic  45.2 us (14%)
  blocking collectives  18.9 us (6%)
  between operations  13.9 us (4%)
  starting transfers between devices  8.82 us (3%)
    all_to_all x1, waiting for transfers between devices, local(): lax.all_to_all(chosen, 'cache', split_axis=0, concat_axis=0, tiled=True)  60.9 us
    dot_general x8, matrix products, add_block(): jnp.einsum('chk,khd->chd', weights, block_values, preferred_element_type=...  37.5 us
    all_gather x2, waiting for transfers between devices, work_in_pieces(): done.append(jax.vmap(apply)(lax.all_gather(piece, axis), starts))  21.2 us
    all_to_all x1, blocking collectives, local(): lax.all_to_all(gated, 'cand', split_axis=0, concat_axis=2, tiled=True)  18.9 us
    unnamed x19, local copies, waits for them, and re-layouts  16.9 us
    dynamic_slice x4, local copies, waits for them, and re-layouts, attend_user(): own = lax.dynamic_index_in_dim(projected, member, 1, keepdims=False)  13.3 us
    dot_general x2, matrix products, project(): jnp.dot(shard_rows.reshape(row_count * users_here, width), proj_matrix, p...  11.2 us
    slice x8, local copies, waits for them, and re-layouts, add_block(): block_keys = piece[:, 0, 0].reshape(block_rows, heads_here, head_size)  10.4 us
  transfers between devices with their start and end apart: 4, of which 3 were waited for; matrix products, arithmetic and copies ran while one was open for 56% of the time, Pallas kernels for 0%

commit v1 on v0

v1 whole, which is shorter than its diff:
```python
import functools

import jax
import jax.numpy as jnp
from jax import lax
from jax.experimental import pallas as pl
from jax.experimental.pallas import tpu as pltpu
from jax.sharding import PartitionSpec as P

EPSILON = 1e-06
MESH = pl.DeviceIdType.MESH
BF16, F32 = jnp.bfloat16, jnp.float32

X = 4
SIDE = 4
CACHE = 2 * SIDE * SIDE
MEMBERS = 2
HEADS_HERE, HD = 2, 128
HW = HEADS_HERE * HD
ROWS = 256
D = 1024
EV = 128
GROUPS, IN_GROUP = 8, 4
BUCKETS = 14
MASKED = -1e30


def silu(x):
    half = x * 0.5
    return half + half * jnp.tanh(half)


def kernel(
    lengths_ref,
    users_ref,
    recency_ref,
    weight_ref,
    cand_hbm,
    win_hbm,
    wout_hbm,
    hist_hbm,
    out_ref,
    scores_ref,
    hist_v,
    send_v,
    arr_v,
    cand_v,
    norm_v,
    win_v,
    wout_v,
    proj_v,
    tot_v,
    gated_v,
    spread_v,
    bias_v,
    local_sem,
    hist_ss,
    hist_rs,
    norm_ss,
    norm_rs,
    wout_ss,
    wout_rs,
    gate_ss,
    gate_rs,
):
    me, mx = lax.axis_index("cache"), lax.axis_index("cand")
    my_y, my_z, my_core = me // (2 * SIDE), (me // 2) % SIDE, me % 2
    scale = HD ** (-0.5)

    def cache_at(group, b, sign):
        a, dc = group // 2, group % 2
        ny = (my_y + sign * b + SIDE) % SIDE
        nz = (my_z + sign * ((a + b) % SIDE) + SIDE) % SIDE
        nc = (my_core + dc) % 2
        return (ny * SIDE + nz) * 2 + nc

    def hist_copy(m, group, b, kv):
        slot = group * IN_GROUP + b
        return pltpu.make_async_remote_copy(
            src_ref=send_v.at[m, slot, kv],
            dst_ref=arr_v.at[m, slot, kv],
            send_sem=hist_ss.at[m, slot, kv],
            recv_sem=hist_rs.at[m, slot, kv],
            device_id={"cache": cache_at(group, b, 1), "cand": mx},
            device_id_type=MESH,
        )

    def norm_copy(m, d):
        return pltpu.make_async_remote_copy(
            src_ref=norm_v.at[m, mx],
            dst_ref=norm_v.at[m, mx],
            send_sem=norm_ss.at[m, d],
            recv_sem=norm_rs.at[m, d],
            device_id={"cache": me, "cand": (mx + d) % X},
            device_id_type=MESH,
        )

    def wout_copy(d):
        return pltpu.make_async_remote_copy(
            src_ref=wout_v.at[mx],
            dst_ref=wout_v.at[mx],
            send_sem=wout_ss.at[d],
            recv_sem=wout_rs.at[d],
            device_id={"cache": me, "cand": (mx + d) % X},
            device_id_type=MESH,
        )

    def gate_copy(m, d):
        return pltpu.make_async_remote_copy(
            src_ref=gated_v.at[m, (mx + d) % X],
            dst_ref=spread_v.at[m, mx],
            send_sem=gate_ss.at[m, d],
            recv_sem=gate_rs.at[m, d],
            device_id={"cache": me, "cand": (mx + d) % X},
            device_id_type=MESH,
        )

    cand_in = pltpu.make_async_copy(cand_hbm, cand_v, local_sem.at[0])
    hist_in = pltpu.make_async_copy(hist_hbm, hist_v, local_sem.at[1])
    win_in = pltpu.make_async_copy(win_hbm, win_v, local_sem.at[2])
    wout_in = pltpu.make_async_copy(wout_hbm, wout_v.at[mx], local_sem.at[3])
    cand_in.start()
    hist_in.start()
    win_in.start()
    wout_in.start()

    barrier = pltpu.get_barrier_semaphore()

    def greet(j, _):
        pl.semaphore_signal(
            barrier,
            inc=1,
            device_id={"cache": (me + j) % CACHE, "cand": mx},
            device_id_type=MESH,
        )
        return 0

    lax.fori_loop(1, CACHE, greet, 0)
    for d in range(1, X):
        pl.semaphore_signal(
            barrier, inc=1, device_id={"cache": me, "cand": (mx + d) % X}, device_id_type=MESH
        )

    cand_in.wait()
    TILE = 32

    def normalize(i, _):
        m, r = i // (ROWS // TILE), i % (ROWS // TILE)
        rows = pl.ds(pl.multiple_of(r * TILE, TILE), TILE)
        x = cand_v[m, rows, :].astype(F32)
        inv = lax.rsqrt(jnp.mean(x * x, axis=-1, keepdims=True) + EPSILON)
        norm_v[m, mx, rows, :] = (x * inv).astype(BF16)
        return 0

    lax.fori_loop(0, MEMBERS * (ROWS // TILE), normalize, 0)
    pl.semaphore_wait(barrier, CACHE - 1 + X - 1)
    for d in (2, 1, 3):
        norm_copy(0, d).start()
    hist_in.wait()

    def gather(m, group):
        for b in range(IN_GROUP):
            user = users_ref[MEMBERS * cache_at(group, b, 1) + m]
            block = hist_v[user]
            slot = group * IN_GROUP + b
            if b == 0:
                own = group == 0

                @pl.when(own)
                def _():
                    arr_v[m, slot] = block

                @pl.when(jnp.logical_not(own))
                def _():
                    send_v[m, slot] = block
            else:
                send_v[m, slot] = block

    def send(m, group):
        for kv in range(2):
            for b in range(IN_GROUP):
                if b == 0:

                    @pl.when(group > 0)
                    def _():
                        hist_copy(m, group, b, kv).start()
                else:
                    hist_copy(m, group, b, kv).start()

    for m in range(MEMBERS):
        gather(m, 0)

        def gather_and_send(group, _):
            @pl.when(group < GROUPS - 1)
            def _():
                gather(m, group + 1)

            send(m, group)
            return 0

        lax.fori_loop(0, GROUPS, gather_and_send, 0)
        if m == 0:
            for d in (2, 1, 3):
                norm_copy(1, d).start()
            wout_in.wait()
            for d in (2, 1, 3):
                wout_copy(d).start()

    lanes = lax.broadcasted_iota(jnp.int32, (1, EV), 1)

    def bias_of(i, _):
        m, group = i // GROUPS, i % GROUPS
        user = users_ref[MEMBERS * me + m]
        length = lengths_ref[user]
        for b in range(IN_GROUP):
            shard = cache_at(group, b, -1)
            position = lax.rem(shard - user + 4 * CACHE, CACHE) * EV + lanes
            distance = jnp.maximum(length - position, 0)
            usable = position < length
            for h in range(HEADS_HERE):
                bias = jnp.full((1, EV), recency_ref[h, 0], F32)
                for k in range(BUCKETS - 1):
                    bias = jnp.where(distance >= 2**k, recency_ref[h, k + 1], bias)
                bias = jnp.where(usable, bias * 0.5, MASKED)
                bias_v[m, h, group, :, b * EV : (b + 1) * EV] = bias
        return 0

    lax.fori_loop(0, MEMBERS * GROUPS, bias_of, 0)
    win_in.wait()

    def project(m):
        def from_source(d, _):
            @pl.when(d > 0)
            def _():
                norm_copy(m, d).wait_recv()

            source = (mx - d + X) % X

            def one_kind(kind, _):
                columns = pl.ds(pl.multiple_of(kind * HW, HW), HW)
                product = jnp.dot(
                    norm_v[m, source], win_v[:, columns], preferred_element_type=F32
                )
                rows = pl.ds(pl.multiple_of(source * ROWS, ROWS), ROWS)
                proj_v[m, kind, rows, :] = silu(product).astype(BF16)
                return 0

            lax.fori_loop(0, 4, one_kind, 0)
            return 0

        lax.fori_loop(0, X, from_source, 0)

        def own_term(t, _):
            rows = pl.ds(pl.multiple_of(t * ROWS, ROWS), ROWS)
            for h in range(HEADS_HERE):
                cols = slice(h * HD, (h + 1) * HD)
                values = proj_v[m, 1, rows, cols].astype(F32)
                queries = proj_v[m, 2, rows, cols].astype(F32)
                keys = proj_v[m, 3, rows, cols].astype(F32)
                score = jnp.sum(queries * keys, axis=-1, keepdims=True) * scale + recency_ref[h, 0]
                tot_v[m, h, rows, :] = silu(score) * values
            return 0

        lax.fori_loop(0, X, own_term, 0)

    def arrived(m, group):
        for b in range(IN_GROUP):
            for kv in range(2):
                if b == 0:

                    @pl.when(group > 0)
                    def _():
                        hist_copy(m, group, b, kv).wait_recv()
                else:
                    hist_copy(m, group, b, kv).wait_recv()

    def attend(m, group, t):
        rows = pl.ds(pl.multiple_of(t * ROWS, ROWS), ROWS)
        slots = pl.ds(group * IN_GROUP, IN_GROUP)
        for h in range(HEADS_HERE):
            cols = slice(h * HD, (h + 1) * HD)
            keys = arr_v[m, slots, 0, :, cols].reshape(IN_GROUP * EV, HD)
            values = arr_v[m, slots, 1, :, cols].reshape(IN_GROUP * EV, HD)
            scores = lax.dot_general(
                proj_v[m, 2, rows, cols],
                keys,
                (((1,), (1,)), ((), ())),
                preferred_element_type=F32,
            )
            half = scores * (0.5 * scale) + bias_v[m, h, group]
            weights = (half + half * jnp.tanh(half)).astype(BF16)
            tot_v[m, h, rows, :] += jnp.dot(weights, values, preferred_element_type=F32)

    def finish(m, d):
        t = (mx + d) % X
        rows = pl.ds(pl.multiple_of(t * ROWS, ROWS), ROWS)
        for h in range(HEADS_HERE):
            cols = slice(h * HD, (h + 1) * HD)
            total = tot_v[m, h, rows, :]
            inv = lax.rsqrt(jnp.mean(total * total, axis=-1, keepdims=True) + EPSILON)
            value = (total * inv * proj_v[m, 0, rows, cols].astype(F32)).astype(BF16)
            if d == 0:
                spread_v[m, mx, :, cols] = value
            else:
                gated_v[m, t, :, cols] = value
        if d != 0:
            gate_copy(m, d).start()

    def attend_groups(m, first, last):
        def step(group, _):
            arrived(m, group)

            def tile(t, _):
                attend(m, group, t)
                return 0

            lax.fori_loop(0, X, tile, 0)
            return 0

        lax.fori_loop(first, last, step, 0)

    def output(m):
        for d in range(1, X):
            gate_copy(m, d).wait_recv()
        partial = jnp.zeros((ROWS, HD), F32)
        wide = 256
        for c in range(D // wide):
            cols = slice(c * wide, (c + 1) * wide)
            total = cand_v[m, :, cols].astype(F32)
            for s in range(X):
                total += jnp.dot(spread_v[m, s], wout_v[s, :, cols], preferred_element_type=F32)
            out_ref[m, :, cols] = total.astype(BF16)
            weighted = total * weight_ref[:, cols]
            for k in range(wide // HD):
                partial += weighted[:, k * HD : (k + 1) * HD]
        scores_ref[m : m + 1, :] = jnp.sum(partial.T, axis=0, keepdims=True)

    project(0)
    attend_groups(0, 0, GROUPS)
    for d in (2, 1, 3, 0):
        finish(0, d)
    project(1)
    attend_groups(1, 0, GROUPS // 2)
    for d in range(1, X):
        wout_copy(d).wait_recv()
    output(0)
    attend_groups(1, GROUPS // 2, GROUPS - 1)
    arrived(1, GROUPS - 1)
    for d in (2, 1, 3, 0):
        attend(1, GROUPS - 1, (mx + d) % X)
        finish(1, d)

    def drain(i, _):
        m, group = i // GROUPS, i % GROUPS
        for b in range(IN_GROUP):
            for kv in range(2):
                if b == 0:

                    @pl.when(group > 0)
                    def _():
                        hist_copy(m, group, b, kv).wait_send()
                else:
                    hist_copy(m, group, b, kv).wait_send()
        return 0

    lax.fori_loop(0, MEMBERS * GROUPS, drain, 0)
    for d in range(1, X):
        norm_copy(0, d).wait_send()
        norm_copy(1, d).wait_send()
        wout_copy(d).wait_send()
        gate_copy(0, d).wait_send()
    output(1)
    for d in range(1, X):
        gate_copy(1, d).wait_send()


def local(cand_states, in_proj, out_proj, history, lengths, rank_users, recency_bias, score_weight):
    members_first = jnp.transpose(cand_states, (1, 0, 2))
    in_matrix = in_proj.reshape(D, 4 * HW)
    stored = history.reshape(history.shape[1:])
    smem = pl.BlockSpec(memory_space=pltpu.SMEM)
    vmem = pl.BlockSpec(memory_space=pltpu.VMEM)
    hbm = pl.BlockSpec(memory_space=pl.ANY)
    dma = pltpu.SemaphoreType.DMA
    out, scores = pl.pallas_call(
        kernel,
        out_shape=(
            jax.ShapeDtypeStruct((MEMBERS, ROWS, D), BF16),
            jax.ShapeDtypeStruct((MEMBERS, ROWS), F32),
        ),
        in_specs=[smem, smem, smem, vmem, hbm, hbm, hbm, hbm],
        out_specs=(vmem, vmem),
        scratch_shapes=[
            pltpu.VMEM(stored.shape, BF16),
            pltpu.VMEM((MEMBERS, CACHE, 2, EV, HW), BF16),
            pltpu.VMEM((MEMBERS, CACHE, 2, EV, HW), BF16),
            pltpu.VMEM((MEMBERS, ROWS, D), BF16),
            pltpu.VMEM((MEMBERS, X, ROWS, D), BF16),
            pltpu.VMEM((D, 4 * HW), BF16),
            pltpu.VMEM((X, HW, D), BF16),
            pltpu.VMEM((MEMBERS, 4, X * ROWS, HW), BF16),
            pltpu.VMEM((MEMBERS, HEADS_HERE, X * ROWS, HD), F32),
            pltpu.VMEM((MEMBERS, X, ROWS, HW), BF16),
            pltpu.VMEM((MEMBERS, X, ROWS, HW), BF16),
            pltpu.VMEM((MEMBERS, HEADS_HERE, GROUPS, 1, IN_GROUP * EV), F32),
            dma((4,)),
            dma((MEMBERS, CACHE, 2)),
            dma((MEMBERS, CACHE, 2)),
            dma((MEMBERS, X)),
            dma((MEMBERS, X)),
            dma((X,)),
            dma((X,)),
            dma((MEMBERS, X)),
            dma((MEMBERS, X)),
        ],
        compiler_params=pltpu.CompilerParams(
            collective_id=0, has_side_effects=True, vmem_limit_bytes=63 << 20
        ),
    )(
        lengths,
        rank_users,
        recency_bias,
        score_weight.reshape(1, D),
        members_first,
        in_matrix,
        out_proj,
        stored,
    )
    return jnp.transpose(out, (1, 0, 2)), scores.T


def solution(mesh):
    in_specs = (
        P("cand", "cache", None),
        P(None, None, "cand"),
        P("cand", None),
        P("cache", None, None, None, "cand"),
        P(),
        P(),
        P("cand", None),
        P(),
    )
    out_specs = (P("cand", "cache", None), P("cand", "cache"))
    return jax.shard_map(local, mesh=mesh, in_specs=in_specs, out_specs=out_specs, check_vma=False)
```

time: 321 us -> 137 us (0.43)
  the two profiles are of different devices: /device:TPU:32 before, /device:TPU:57 now
where the time goes in v1:
time: 137 us
  Pallas kernels  128 us (93%)
  local copies, waits for them, and re-layouts  8.31 us (6%)
    pallas_call x1, Pallas kernels, local(): pl.pallas_call(kernel, out_shape=(jax.ShapeDtypeStruct((MEMBERS, ROWS, D)...  128 us
    unnamed x8, local copies, waits for them, and re-layouts  8.31 us

profile of v1, /device:TPU:57, one launch (start us, length us, event | category | flops | bytes accessed | tf_op | source)
XLA Modules:
  0.0 136.9 jit_solution(17881763838735394572)
XLA Ops:
  0.6 0.0 copy-start
  0.6 2.6 %copy.14 = bf16[256,2,1024]{2,0,1:T(8,128)(2,1)} copy(bf16[256,2,1024]{2,1,0:T(2,128)(2,1)} %param.8) | data formatting | bytes 2097152 | tf_op args[0]
  3.3 0.0 copy-done
  3.3 1.8 %copy.12 = bf16[128,8,4,256]{3,1,2,0:T(8,128)(2,1)} copy(bf16[128,8,4,256]{3,2,1,0:T(4,128)(2,1)S(1)} %bitcast.12) | data formatting | bytes 4194304
  5.1 128.0 %shard_map.95 = (bf16[2,256,1024]{2,1,0:T(8,128)(2,1)}, f32[2,256]{1,0:T(2,128)}) custom-call(s32[64]{0:T(128)} %lengths_ref.1, s32[64]{0:T(128)} %users_ref.1, f32[2,14]{1,0:T(2,128)} %recency_ref.1, f32[1,1024]{1,0:T(1,128)} %bitcast.14, bf16[2,256,1024]{2,1,0:T(8,128)(2,1)} %bitcast.11, bf16[1024,1024]{1,0:T(8,128)(2,1)} %bitcast.10, ...), custom_call_target="tpu_custom_call" | custom-call | tf_op jit(solution)/shard_map/pallas_call | solution.py:385
  133.1 0.0 copy-start.1
  133.1 3.3 %copy.11 = bf16[256,2,1024]{2,1,0:T(2,128)(2,1)} copy(bf16[256,2,1024]{2,0,1:T(8,128)(2,1)} %bitcast.13) | data formatting | bytes 2097152
  136.4 0.0 copy-done.1
  136.4 0.6 copy.16
Async XLA Ops:
  0.6 2.6 %copy-start = (bf16[1024,4,256]{2,1,0:T(4,128)(2,1)S(1)}, bf16[1024,4,256]{2,1,0:T(4,128)(2,1)}, u32[]{:S(2)}) copy-start(bf16[1024,4,256]{2,1,0:T(4,128)(2,1)} %param.9) | copy-start | bytes 6291460
  133.1 3.3 %copy-start.1 = (f32[2,256]{1,0:T(2,128)S(1)}, f32[2,256]{1,0:T(2,128)}, u32[]{:S(2)}) copy-start(f32[2,256]{1,0:T(2,128)} %get-tuple-element.5) | copy-start | bytes 6148

commit v2 on v1

--- a/solution.py
+++ b/solution.py
@@ -22,6 +22,7 @@
 EV = 128
 GROUPS, IN_GROUP = 8, 4
 BUCKETS = 14
+AHEAD = 6
 MASKED = -1e30
 
 
@@ -187,24 +188,28 @@
                 else:
                     hist_copy(m, group, b, kv).start()
 
-    for m in range(MEMBERS):
-        gather(m, 0)
-
-        def gather_and_send(group, _):
-            @pl.when(group < GROUPS - 1)
-            def _():
-                gather(m, group + 1)
-
-            send(m, group)
-            return 0
-
-        lax.fori_loop(0, GROUPS, gather_and_send, 0)
-        if m == 0:
-            for d in (2, 1, 3):
-                norm_copy(1, d).start()
-            wout_in.wait()
-            for d in (2, 1, 3):
-                wout_copy(d).start()
+    gather(0, 0)
+
+    def gather_and_send(group, _):
+        @pl.when(group < GROUPS - 1)
+        def _():
+            gather(0, group + 1)
+
+        send(0, group)
+        return 0
+
+    lax.fori_loop(0, GROUPS, gather_and_send, 0)
+    for d in (2, 1, 3):
+        norm_copy(1, d).start()
+    wout_in.wait()
+    for d in (2, 1, 3):
+        wout_copy(d).start()
+
+    def gather_next(group, _):
+        gather(1, group)
+        return 0
+
+    lax.fori_loop(0, GROUPS, gather_next, 0)
 
     lanes = lax.broadcasted_iota(jnp.int32, (1, EV), 1)
 
@@ -273,6 +278,17 @@
                         hist_copy(m, group, b, kv).wait_recv()
                 else:
                     hist_copy(m, group, b, kv).wait_recv()
+
+    def sent(m, group):
+        for b in range(IN_GROUP):
+            for kv in range(2):
+                if b == 0:
+
+                    @pl.when(group > 0)
+                    def _():
+                        hist_copy(m, group, b, kv).wait_send()
+                else:
+                    hist_copy(m, group, b, kv).wait_send()
 
     def attend(m, group, t):
         rows = pl.ds(pl.multiple_of(t * ROWS, ROWS), ROWS)
@@ -309,6 +325,18 @@
     def attend_groups(m, first, last):
         def step(group, _):
             arrived(m, group)
+            if m == 0:
+                sent(0, group)
+
+                @pl.when(group + AHEAD >= GROUPS)
+                def _():
+                    send(1, group + AHEAD - GROUPS)
+            else:
+
+                @pl.when(group + AHEAD < GROUPS)
+                def _():
+                    sent(1, group)
+                    send(1, group + AHEAD)
 
             def tile(t, _):
                 attend(m, group, t)
@@ -350,20 +378,11 @@
         attend(1, GROUPS - 1, (mx + d) % X)
         finish(1, d)
 
-    def drain(i, _):
-        m, group = i // GROUPS, i % GROUPS
-        for b in range(IN_GROUP):
-            for kv in range(2):
-                if b == 0:
-
-                    @pl.when(group > 0)
-                    def _():
-                        hist_copy(m, group, b, kv).wait_send()
-                else:
-                    hist_copy(m, group, b, kv).wait_send()
-        return 0
-
-    lax.fori_loop(0, MEMBERS * GROUPS, drain, 0)
+    def drain(group, _):
+        sent(1, group)
+        return 0
+
+    lax.fori_loop(GROUPS - AHEAD, GROUPS, drain, 0)
     for d in range(1, X):
         norm_copy(0, d).wait_send()
         norm_copy(1, d).wait_send()

time: 137 us -> 133 us (0.971)
  the two profiles are of different devices: /device:TPU:57 before, /device:TPU:1 now
where the time goes in v2:
time: 133 us
  Pallas kernels  124 us (93%)
  local copies, waits for them, and re-layouts  8.31 us (6%)
    pallas_call x1, Pallas kernels, local(): pl.pallas_call(kernel, out_shape=(jax.ShapeDtypeStruct((MEMBERS, ROWS, D)...  124 us
    unnamed x8, local copies, waits for them, and re-layouts  8.31 us

profile of v2, /device:TPU:1, one launch (start us, length us, event | category | flops | bytes accessed | tf_op | source)
XLA Modules:
  0.0 132.7 jit_solution(12750777188168136499)
XLA Ops:
  0.6 0.0 copy-start
  0.6 2.6 %copy.14 = bf16[256,2,1024]{2,0,1:T(8,128)(2,1)} copy(bf16[256,2,1024]{2,1,0:T(2,128)(2,1)} %param.8) | data formatting | bytes 2097152 | tf_op args[0]
  3.3 0.0 copy-done
  3.3 1.8 %copy.12 = bf16[128,8,4,256]{3,1,2,0:T(8,128)(2,1)} copy(bf16[128,8,4,256]{3,2,1,0:T(4,128)(2,1)S(1)} %bitcast.12) | data formatting | bytes 4194304
  5.1 123.7 %shard_map.95 = (bf16[2,256,1024]{2,1,0:T(8,128)(2,1)}, f32[2,256]{1,0:T(2,128)}) custom-call(s32[64]{0:T(128)} %lengths_ref.1, s32[64]{0:T(128)} %users_ref.1, f32[2,14]{1,0:T(2,128)} %recency_ref.1, f32[1,1024]{1,0:T(1,128)} %bitcast.14, bf16[2,256,1024]{2,1,0:T(8,128)(2,1)} %bitcast.11, bf16[1024,1024]{1,0:T(8,128)(2,1)} %bitcast.10, ...), custom_call_target="tpu_custom_call" | custom-call | tf_op jit(solution)/shard_map/pallas_call | solution.py:404
  128.8 0.0 copy-start.1
  128.8 3.3 %copy.11 = bf16[256,2,1024]{2,1,0:T(2,128)(2,1)} copy(bf16[256,2,1024]{2,0,1:T(8,128)(2,1)} %bitcast.13) | data formatting | bytes 2097152
  132.1 0.0 copy-done.1
  132.1 0.6 copy.16
Async XLA Ops:
  0.6 2.6 %copy-start = (bf16[1024,4,256]{2,1,0:T(4,128)(2,1)S(1)}, bf16[1024,4,256]{2,1,0:T(4,128)(2,1)}, u32[]{:S(2)}) copy-start(bf16[1024,4,256]{2,1,0:T(4,128)(2,1)} %param.9) | copy-start | bytes 6291460
  128.8 3.3 %copy-start.1 = (f32[2,256]{1,0:T(2,128)S(1)}, f32[2,256]{1,0:T(2,128)}, u32[]{:S(2)}) copy-start(f32[2,256]{1,0:T(2,128)} %get-tuple-element.5) | copy-start | bytes 6148

commit v3 on v2

--- a/solution.py
+++ b/solution.py
@@ -23,6 +23,8 @@
 GROUPS, IN_GROUP = 8, 4
 BUCKETS = 14
 AHEAD = 6
+BIAS_LANES = 16
+FAR = 1 << 30
 MASKED = -1e30
 
 
@@ -53,6 +55,7 @@
     tot_v,
     gated_v,
     spread_v,
+    onehot_v,
     bias_v,
     local_sem,
     hist_ss,
@@ -211,26 +214,41 @@
 
     lax.fori_loop(0, GROUPS, gather_next, 0)
 
-    lanes = lax.broadcasted_iota(jnp.int32, (1, EV), 1)
-
-    def bias_of(i, _):
+    lane = lax.broadcasted_iota(jnp.int32, (1, HD), 1)
+    bucket = jnp.where(lane < 3 * BIAS_LANES, lane % BIAS_LANES, 0)
+    low = jnp.full((1, HD), FAR, jnp.int32)
+    high = jnp.full((1, HD), FAR, jnp.int32)
+    for k in range(1, BUCKETS):
+        low = jnp.where(bucket == k, 2 ** (k - 1), low)
+        high = jnp.where(bucket == k, FAR if k == BUCKETS - 1 else 2**k, high)
+    low = jnp.where(bucket == BUCKETS, -FAR, low)
+    high = jnp.where(bucket == BUCKETS, 1, high)
+    for h in range(HEADS_HERE):
+        bias = jnp.zeros((1, HD), F32)
+        for k in range(1, BUCKETS):
+            bias = jnp.where(bucket == k, recency_ref[h, k] * 0.5, bias)
+        first = bias.astype(BF16).astype(F32)
+        second = (bias - first).astype(BF16).astype(F32)
+        third = bias - first - second
+        row = jnp.where(lane < 2 * BIAS_LANES, second, third)
+        row = jnp.where(lane < BIAS_LANES, first, row)
+        row = jnp.where(lane == BUCKETS, MASKED, row)
+        bias_v[h] = jnp.broadcast_to(row, (ROWS, HD)).astype(BF16)
+    event = lax.broadcasted_iota(jnp.int32, (EV, HD), 0)
+
+    def buckets_of(i, _):
         m, group = i // GROUPS, i % GROUPS
         user = users_ref[MEMBERS * me + m]
         length = lengths_ref[user]
         for b in range(IN_GROUP):
             shard = cache_at(group, b, -1)
-            position = lax.rem(shard - user + 4 * CACHE, CACHE) * EV + lanes
-            distance = jnp.maximum(length - position, 0)
-            usable = position < length
-            for h in range(HEADS_HERE):
-                bias = jnp.full((1, EV), recency_ref[h, 0], F32)
-                for k in range(BUCKETS - 1):
-                    bias = jnp.where(distance >= 2**k, recency_ref[h, k + 1], bias)
-                bias = jnp.where(usable, bias * 0.5, MASKED)
-                bias_v[m, h, group, :, b * EV : (b + 1) * EV] = bias
-        return 0
-
-    lax.fori_loop(0, MEMBERS * GROUPS, bias_of, 0)
+            start = lax.rem(shard - user + 4 * CACHE, CACHE) * EV
+            distance = (length - start) - event
+            hit = (distance >= low) & (distance < high)
+            onehot_v[m, group * IN_GROUP + b] = jnp.where(hit, 1.0, 0.0).astype(BF16)
+        return 0
+
+    lax.fori_loop(0, MEMBERS * GROUPS, buckets_of, 0)
     win_in.wait()
 
     def project(m):
@@ -247,7 +265,8 @@
                     norm_v[m, source], win_v[:, columns], preferred_element_type=F32
                 )
                 rows = pl.ds(pl.multiple_of(source * ROWS, ROWS), ROWS)
-                proj_v[m, kind, rows, :] = silu(product).astype(BF16)
+                factor = jnp.where(kind == 2, 0.5 * scale, 1.0)
+                proj_v[m, kind, rows, :] = (silu(product) * factor).astype(BF16)
                 return 0
 
             lax.fori_loop(0, 4, one_kind, 0)
@@ -262,8 +281,8 @@
                 values = proj_v[m, 1, rows, cols].astype(F32)
                 queries = proj_v[m, 2, rows, cols].astype(F32)
                 keys = proj_v[m, 3, rows, cols].astype(F32)
-                score = jnp.sum(queries * keys, axis=-1, keepdims=True) * scale + recency_ref[h, 0]
-                tot_v[m, h, rows, :] = silu(score) * values
+                half = jnp.sum(queries * keys, axis=-1, keepdims=True) + recency_ref[h, 0] * 0.5
+                tot_v[m, h, rows, :] = (half + half * jnp.tanh(half)) * values
             return 0
 
         lax.fori_loop(0, X, own_term, 0)
@@ -297,13 +316,13 @@
             cols = slice(h * HD, (h + 1) * HD)
             keys = arr_v[m, slots, 0, :, cols].reshape(IN_GROUP * EV, HD)
             values = arr_v[m, slots, 1, :, cols].reshape(IN_GROUP * EV, HD)
-            scores = lax.dot_general(
-                proj_v[m, 2, rows, cols],
-                keys,
+            near = onehot_v[m, slots].reshape(IN_GROUP * EV, HD)
+            half = lax.dot_general(
+                jnp.concatenate([proj_v[m, 2, rows, cols], bias_v[h]], axis=1),
+                jnp.concatenate([keys, near], axis=1),
                 (((1,), (1,)), ((), ())),
                 preferred_element_type=F32,
             )
-            half = scores * (0.5 * scale) + bias_v[m, h, group]
             weights = (half + half * jnp.tanh(half)).astype(BF16)
             tot_v[m, h, rows, :] += jnp.dot(weights, values, preferred_element_type=F32)
 
@@ -421,7 +440,8 @@
             pltpu.VMEM((MEMBERS, HEADS_HERE, X * ROWS, HD), F32),
             pltpu.VMEM((MEMBERS, X, ROWS, HW), BF16),
             pltpu.VMEM((MEMBERS, X, ROWS, HW), BF16),
-            pltpu.VMEM((MEMBERS, HEADS_HERE, GROUPS, 1, IN_GROUP * EV), F32),
+            pltpu.VMEM((MEMBERS, CACHE, EV, HD), BF16),
+            pltpu.VMEM((HEADS_HERE, ROWS, HD), BF16),
             dma((4,)),
             dma((MEMBERS, CACHE, 2)),
             dma((MEMBERS, CACHE, 2)),

time: 133 us -> 133 us (level)
  no operation moved by 1% of the time
where the time goes in v3:
time: 133 us
  Pallas kernels  124 us (93%)
  local copies, waits for them, and re-layouts  8.31 us (6%)
    pallas_call x1, Pallas kernels, local(): pl.pallas_call(kernel, out_shape=(jax.ShapeDtypeStruct((MEMBERS, ROWS, D)...  124 us
    unnamed x8, local copies, waits for them, and re-layouts  8.31 us

profile of v3, /device:TPU:1, one launch (start us, length us, event | category | flops | bytes accessed | tf_op | source)
XLA Modules:
  0.0 132.6 jit_solution(551977185707188280)
XLA Ops:
  0.6 0.0 copy-start
  0.6 2.6 %copy.14 = bf16[256,2,1024]{2,0,1:T(8,128)(2,1)} copy(bf16[256,2,1024]{2,1,0:T(2,128)(2,1)} %param.8) | data formatting | bytes 2097152 | tf_op args[0]
  3.3 0.0 copy-done
  3.3 1.8 %copy.12 = bf16[128,8,4,256]{3,1,2,0:T(8,128)(2,1)} copy(bf16[128,8,4,256]{3,2,1,0:T(4,128)(2,1)S(1)} %bitcast.12) | data formatting | bytes 4194304
  5.1 123.7 %shard_map.95 = (bf16[2,256,1024]{2,1,0:T(8,128)(2,1)}, f32[2,256]{1,0:T(2,128)}) custom-call(s32[64]{0:T(128)} %lengths_ref.1, s32[64]{0:T(128)} %users_ref.1, f32[2,14]{1,0:T(2,128)} %recency_ref.1, f32[1,1024]{1,0:T(1,128)} %bitcast.14, bf16[2,256,1024]{2,1,0:T(8,128)(2,1)} %bitcast.11, bf16[1024,1024]{1,0:T(8,128)(2,1)} %bitcast.10, ...), custom_call_target="tpu_custom_call" | custom-call | tf_op jit(solution)/shard_map/pallas_call | solution.py:423
  128.8 0.0 copy-start.1
  128.8 3.3 %copy.11 = bf16[256,2,1024]{2,1,0:T(2,128)(2,1)} copy(bf16[256,2,1024]{2,0,1:T(8,128)(2,1)} %bitcast.13) | data formatting | bytes 2097152
  132.0 0.0 copy-done.1
  132.0 0.6 copy.16
Async XLA Ops:
  0.6 2.6 %copy-start = (bf16[1024,4,256]{2,1,0:T(4,128)(2,1)S(1)}, bf16[1024,4,256]{2,1,0:T(4,128)(2,1)}, u32[]{:S(2)}) copy-start(bf16[1024,4,256]{2,1,0:T(4,128)(2,1)} %param.9) | copy-start | bytes 6291460
  128.8 3.3 %copy-start.1 = (f32[2,256]{1,0:T(2,128)S(1)}, f32[2,256]{1,0:T(2,128)}, u32[]{:S(2)}) copy-start(f32[2,256]{1,0:T(2,128)} %get-tuple-element.5) | copy-start | bytes 6148

commit v4 on v2

--- a/solution.py
+++ b/solution.py
@@ -120,8 +120,8 @@
     hist_in = pltpu.make_async_copy(hist_hbm, hist_v, local_sem.at[1])
     win_in = pltpu.make_async_copy(win_hbm, win_v, local_sem.at[2])
     wout_in = pltpu.make_async_copy(wout_hbm, wout_v.at[mx], local_sem.at[3])
+    hist_in.start()
     cand_in.start()
-    hist_in.start()
     win_in.start()
     wout_in.start()
 
@@ -142,21 +142,7 @@
             barrier, inc=1, device_id={"cache": me, "cand": (mx + d) % X}, device_id_type=MESH
         )
 
-    cand_in.wait()
-    TILE = 32
-
-    def normalize(i, _):
-        m, r = i // (ROWS // TILE), i % (ROWS // TILE)
-        rows = pl.ds(pl.multiple_of(r * TILE, TILE), TILE)
-        x = cand_v[m, rows, :].astype(F32)
-        inv = lax.rsqrt(jnp.mean(x * x, axis=-1, keepdims=True) + EPSILON)
-        norm_v[m, mx, rows, :] = (x * inv).astype(BF16)
-        return 0
-
-    lax.fori_loop(0, MEMBERS * (ROWS // TILE), normalize, 0)
     pl.semaphore_wait(barrier, CACHE - 1 + X - 1)
-    for d in (2, 1, 3):
-        norm_copy(0, d).start()
     hist_in.wait()
 
     def gather(m, group):
@@ -199,8 +185,21 @@
         return 0
 
     lax.fori_loop(0, GROUPS, gather_and_send, 0)
-    for d in (2, 1, 3):
-        norm_copy(1, d).start()
+    cand_in.wait()
+    TILE = 32
+
+    def normalize(i, _):
+        m, r = i // (ROWS // TILE), i % (ROWS // TILE)
+        rows = pl.ds(pl.multiple_of(r * TILE, TILE), TILE)
+        x = cand_v[m, rows, :].astype(F32)
+        inv = lax.rsqrt(jnp.mean(x * x, axis=-1, keepdims=True) + EPSILON)
+        norm_v[m, mx, rows, :] = (x * inv).astype(BF16)
+        return 0
+
+    lax.fori_loop(0, MEMBERS * (ROWS // TILE), normalize, 0)
+    for m in range(MEMBERS):
+        for d in (2, 1, 3):
+            norm_copy(m, d).start()
     wout_in.wait()
     for d in (2, 1, 3):
         wout_copy(d).start()

time: 133 us -> 128 us (0.962)
  Pallas kernels: 124 us -> 118 us
    pallas_call x1, Pallas kernels: 124 us -> 118 us  [local(): pl.pallas_call(kernel, out_shape=(jax.ShapeDtypeStruct((MEMBERS, ROWS, D)...]
where the time goes in v4:
time: 128 us; the launch traced here: 127 us
  Pallas kernels  118 us (92%)
  local copies, waits for them, and re-layouts  8.31 us (6%)
    pallas_call x1, Pallas kernels, local(): pl.pallas_call(kernel, out_shape=(jax.ShapeDtypeStruct((MEMBERS, ROWS, D)...  118 us
    unnamed x8, local copies, waits for them, and re-layouts  8.31 us

profile of v4, /device:TPU:1, one launch (start us, length us, event | category | flops | bytes accessed | tf_op | source)
XLA Modules:
  0.0 126.6 jit_solution(1229822001116449735)
XLA Ops:
  0.6 0.0 copy-start
  0.6 2.6 %copy.14 = bf16[256,2,1024]{2,0,1:T(8,128)(2,1)} copy(bf16[256,2,1024]{2,1,0:T(2,128)(2,1)} %param.8) | data formatting | bytes 2097152 | tf_op args[0]
  3.3 0.0 copy-done
  3.3 1.8 %copy.12 = bf16[128,8,4,256]{3,1,2,0:T(8,128)(2,1)} copy(bf16[128,8,4,256]{3,2,1,0:T(4,128)(2,1)S(1)} %bitcast.12) | data formatting | bytes 4194304
  5.1 117.6 %shard_map.95 = (bf16[2,256,1024]{2,1,0:T(8,128)(2,1)}, f32[2,256]{1,0:T(2,128)}) custom-call(s32[64]{0:T(128)} %lengths_ref.1, s32[64]{0:T(128)} %users_ref.1, f32[2,14]{1,0:T(2,128)} %recency_ref.1, f32[1,1024]{1,0:T(1,128)} %bitcast.14, bf16[2,256,1024]{2,1,0:T(8,128)(2,1)} %bitcast.11, bf16[1024,1024]{1,0:T(8,128)(2,1)} %bitcast.10, ...), custom_call_target="tpu_custom_call" | custom-call | tf_op jit(solution)/shard_map/pallas_call | solution.py:403
  122.7 0.0 copy-start.1
  122.7 3.3 %copy.11 = bf16[256,2,1024]{2,1,0:T(2,128)(2,1)} copy(bf16[256,2,1024]{2,0,1:T(8,128)(2,1)} %bitcast.13) | data formatting | bytes 2097152
  126.0 0.0 copy-done.1
  126.0 0.6 copy.16
Async XLA Ops:
  0.6 2.6 %copy-start = (bf16[1024,4,256]{2,1,0:T(4,128)(2,1)S(1)}, bf16[1024,4,256]{2,1,0:T(4,128)(2,1)}, u32[]{:S(2)}) copy-start(bf16[1024,4,256]{2,1,0:T(4,128)(2,1)} %param.9) | copy-start | bytes 6291460
  122.7 3.3 %copy-start.1 = (f32[2,256]{1,0:T(2,128)S(1)}, f32[2,256]{1,0:T(2,128)}, u32[]{:S(2)}) copy-start(f32[2,256]{1,0:T(2,128)} %get-tuple-element.5) | copy-start | bytes 6148
